TPU v7x, 32 devices: a whole 2x2x4 slice. The times are simulated.
32 devices in a mesh: clip: 2 (over x), space: 4 (over y, core), tm: 4 (over z).
Axes of the slice: x: 2, y: 2, z: 4, core: 2. Of those that a mesh axis runs over, the one named last changes fastest.
Arguments:
- block_input: bfloat16 [8, 12, 160, 384], P(('clip', 'tm'), 'space'), parts along dimension 0, may hold values from -24 to 24, as said below
- conv_input: bfloat16 [8, 12, 160, 384], P(('clip', 'tm'), 'space'), parts along dimension 0, may hold values from -24 to 24, as said below
- norm_gain: float32 [384], replicated, may hold values from 0.1 to 1.9
- norm_bias: float32 [384], replicated, may hold values from -3 to 3
- conv_weight: bfloat16 [3, 3, 3, 384, 384], replicated, may hold values from -0.0625 to 0.0625
- conv_bias: float32 [384], replicated, may hold values from -1.5 to 1.5
- attn_gain: float32 [384], replicated, may hold values from 0.1 to 1.9
- attn_bias: float32 [384], replicated, may hold values from -1.5 to 1.5
- query_weight: bfloat16 [384, 384], replicated, may hold values from -4 to 4
- query_bias: float32 [384], replicated, may hold values from -1.5 to 1.5
- key_weight: bfloat16 [384, 384], replicated, may hold values from -4 to 4
- value_weight: bfloat16 [384, 384], replicated, may hold values from -0.3125 to 0.3125
- value_bias: float32 [384], replicated, may hold values from -3 to 3
- out_weight: bfloat16 [384, 384], replicated, may hold values from -0.3125 to 0.3125
- out_bias: float32 [384], replicated, may hold values from -3 to 3
Outputs:
- block_output: bfloat16 [8, 12, 160, 384], P(('clip', 'tm'), 'space'), parts along dimension 0
There are 2 independent parts, one for each index of `clip`. A program takes and returns all parts, laid end to end along the dimension named above; an argument that names none is the same for every part. Nothing has to cross between parts.
Inputs may be any that keep to these rules, and one draw needn't show every extreme that they name: `block_input`: finite activations. `conv_input`: finite activations.
All inputs are finite; a program needn't handle non-finite values.
Results may differ from a plain program's by a relative error of at most 0.0075.
Values may be sent and summed in bfloat16 or wider, within the bound.
No kernel may reach another device: no remote copies, remote signals or barrier semaphores. Data moves between devices by JAX's collectives and lax.ppermute only.
A program may use at most 128 MiB of HBM per device.

v0:
```python
import jax
import jax.numpy as jnp
from jax import lax
from jax.sharding import PartitionSpec as P


def from_behind(value, axis, steps):
    count = lax.axis_size(axis)
    leading, last = (max(0, -steps), min(count, count - steps))
    return lax.ppermute(value, axis, [(source, source + steps) for source in range(leading, last)])


def padded_2(x, sides, width):
    for axis, dim in sides:
        peers, length = (lax.axis_size(axis), x.shape[dim])
        up = [(i, (i + 1) % peers) for i in range(peers - 1)]
        down = [(j, i) for i, j in up]
        last = lax.slice_in_dim(x, length - width, length, axis=dim)
        leading = lax.slice_in_dim(x, 0, width, axis=dim)
        before = lax.ppermute(last, axis, up)
        after = lax.ppermute(leading, axis, down)
        x = jnp.concatenate([before, x, after], axis=dim)
    return x


def rms_norm(field, gain, bias):
    mean_square = jnp.mean(field * field, axis=-1, keepdims=True)
    return field * lax.rsqrt(mean_square + 1e-06) * gain + bias


def causal_conv(padded, conv_weight, frame_count, row_count, columns):
    channels = padded.shape[-1]
    running = jnp.zeros((frame_count * row_count * columns, channels), jnp.float32)
    for tap_t in range(3):
        for tap_y in range(3):
            window = padded[tap_t : tap_t + frame_count, tap_y : tap_y + row_count]
            joined = jnp.concatenate(
                [window[:, :, tap_x : tap_x + columns] for tap_x in range(3)], axis=-1
            )
            joined = joined.reshape(-1, 3 * channels)
            kernel = conv_weight[tap_t, tap_y].reshape(3 * channels, channels)
            running = running + jnp.dot(joined, kernel, preferred_element_type=jnp.float32)
    return running.reshape(frame_count, row_count, columns, channels)


def absorb(state, queries, key_rows, value_rows, score_scale):
    numer_acc, denom_acc, max_acc = state
    scores = (
        jnp.einsum("fqc,fkc->fqk", queries, key_rows, preferred_element_type=jnp.float32)
        * score_scale
    )
    new_max = jnp.maximum(max_acc, jnp.max(scores, axis=-1))
    expd = jnp.exp(scores - new_max[..., None])
    weights = expd.astype(jnp.bfloat16)
    added = jnp.einsum("fqk,fkc->fqc", weights, value_rows, preferred_element_type=jnp.float32)
    numer_acc = added
    denom_acc = jnp.sum(expd, axis=-1)
    return (numer_acc, denom_acc, new_max)


def shards(
    block_input,
    conv_input,
    norm_gain,
    norm_bias,
    conv_weight,
    conv_bias,
    attn_gain,
    attn_bias,
    query_weight,
    query_bias,
    key_weight,
    value_weight,
    value_bias,
    out_weight,
    out_bias,
):
    frame_count, row_count, columns, channels = block_input.shape
    field = conv_input.astype(jnp.float32)
    activated = jax.nn.silu(rms_norm(field, norm_gain, norm_bias)).astype(jnp.bfloat16)
    earlier = [from_behind(activated, "tm", offset) for offset in (1, 2)]
    stacked = jnp.concatenate([earlier[1], earlier[0], activated], axis=0)
    padded = padded_2(stacked, (("space", 1),), 1)
    padded = jnp.pad(padded, ((0, 0), (0, 0), (1, 1), (0, 0)))
    convolved = causal_conv(padded, conv_weight, frame_count, row_count, columns) + conv_bias
    mixed = (block_input.astype(jnp.float32) + convolved).astype(jnp.bfloat16)
    mixed_wide = mixed.astype(jnp.float32)
    normed = rms_norm(mixed_wide, attn_gain, attn_bias).astype(jnp.bfloat16)
    flat_rows = normed.reshape(frame_count, row_count * columns, channels)
    score_scale = float(channels) ** (-0.5)
    queries = (
        jnp.dot(flat_rows, query_weight, preferred_element_type=jnp.float32) + query_bias
    ).astype(jnp.bfloat16)
    query_count = row_count * columns
    start_state = (
        jnp.zeros((frame_count, query_count, channels), jnp.float32),
        jnp.zeros((frame_count, query_count), jnp.float32),
        jnp.full((frame_count, query_count), -1e30, jnp.float32),
    )
    source = lax.all_gather(normed, "space", axis=1, tiled=True).reshape(frame_count, -1, channels)
    key_rows = jnp.dot(source, key_weight, preferred_element_type=jnp.float32).astype(jnp.bfloat16)
    value_rows = (
        jnp.dot(source, value_weight, preferred_element_type=jnp.float32) + value_bias
    ).astype(jnp.bfloat16)
    numer_acc, denom_acc, max_acc = absorb(start_state, queries, key_rows, value_rows, score_scale)
    attended = (numer_acc / denom_acc[..., None]).astype(jnp.bfloat16)
    projected = jnp.dot(attended, out_weight, preferred_element_type=jnp.float32) + out_bias
    return (mixed_wide + projected.reshape(mixed_wide.shape)).astype(jnp.bfloat16)


def solution(mesh):
    placed = (
        P(("clip", "tm"), "space", None, None),
        P(("clip", "tm"), "space", None, None),
        P(),
        P(),
        P(),
        P(),
        P(),
        P(),
        P(),
        P(),
        P(),
        P(),
        P(),
        P(),
        P(),
    )
    return jax.shard_map(
        shards,
        mesh=mesh,
        in_specs=placed,
        out_specs=P(("clip", "tm"), "space", None, None),
        check_vma=False,
    )
```

profile of v0, /device:TPU:0, one launch (start us, length us, event | category | flops | bytes accessed | tf_op | source)
XLA Modules:
  0.0 103.6 jit_solution(10755714841860632833)
XLA Ops:
  6.5 1.2 %fusion.35 = f32[3,160]{1,0:T(4,128)S(1)} fusion(bf16[1,3,160,384]{3,2,1,0:T(8,128)(2,1)} %param.16), kind=kLoop, calls=%fused_computation.72 | loop fusion | flops 552480 | bytes 370560 | tf_op jit(solution)/shard_map/reduce_sum | solution.py:27
  7.8 1.3 %fusion.43 = bf16[1,3,160,384]{3,2,1,0:T(8,128)(2,1)S(1)} fusion(bf16[1,3,160,384]{3,2,1,0:T(8,128)(2,1)} %param.16, f32[384]{0:T(512)} %param.18, f32[384]{0:T(512)} %param.17, f32[3,160]{1,0:T(4,128)S(1)} %add_rsqrt_fusion.1), kind=kLoop, calls=%fused_computation.80 | loop fusion | flops 1658880 | bytes 742272 | tf_op jit(solution)/shard_map/convert_element_type | solution.py:80
  9.1 5.0 %collective-permute-start.1 = (bf16[1,3,160,384]{3,2,1,0:T(8,128)(2,1)S(1)}, bf16[1,3,160,384]{3,2,1,0:T(8,128)(2,1)S(1)}, u32[]{:S(2)}, u32[]{:S(2)}) collective-permute-start(bf16[1,3,160,384]{3,2,1,0:T(8,128)(2,1)S(1)} %fusion.43), channel_id=1, source_target_pairs={{0,1},{1,2},{2,3},{4,5},{5,6},{6,7},{8,9},{9,10},{10,11},{12,13},{... | collective-permute-start | bytes 1105928 | tf_op jit(solution)/shard_map/ppermute | solution.py:10
  14.1 4.5 %collective-permute-start = (bf16[1,3,160,384]{3,2,1,0:T(8,128)(2,1)S(1)}, bf16[1,3,160,384]{3,2,1,0:T(8,128)(2,1)S(1)}, u32[]{:S(2)}, u32[]{:S(2)}) collective-permute-start(bf16[1,3,160,384]{3,2,1,0:T(8,128)(2,1)S(1)} %fusion.43), channel_id=1, source_target_pairs={{0,2},{1,3},{4,6},{5,7},{8,10},{9,11},{12,14},{13,15},{16,18},{17,... | collective-permute-start | bytes 1105928 | tf_op jit(solution)/shard_map/ppermute | solution.py:10
  18.6 4.4 %collective-permute-done.1 = bf16[1,3,160,384]{3,2,1,0:T(8,128)(2,1)S(1)} collective-permute-done((bf16[1,3,160,384]{3,2,1,0:T(8,128)(2,1)S(1)}, bf16[1,3,160,384]{3,2,1,0:T(8,128)(2,1)S(1)}, u32[]{:S(2)}, u32[]{:S(2)}) %collective-permute-start.1) | collective-permute-done | bytes 368672 | tf_op jit(solution)/shard_map/ppermute | solution.py:10
  23.0 6.8 %collective-permute-done = bf16[1,3,160,384]{3,2,1,0:T(8,128)(2,1)S(1)} collective-permute-done((bf16[1,3,160,384]{3,2,1,0:T(8,128)(2,1)S(1)}, bf16[1,3,160,384]{3,2,1,0:T(8,128)(2,1)S(1)}, u32[]{:S(2)}, u32[]{:S(2)}) %collective-permute-start) | collective-permute-done | bytes 368672 | tf_op jit(solution)/shard_map/ppermute | solution.py:10
  29.9 1.3 %collective-permute-start.2 = (bf16[3,1,160,384]{3,2,1,0:T(8,128)(2,1)S(1)}, bf16[3,1,160,384]{3,2,1,0:T(8,128)(2,1)S(1)}, u32[]{:S(2)}, u32[]{:S(2)}) collective-permute-start(bf16[3,1,160,384]{3,2,1,0:T(8,128)(2,1)S(1)} %get-tuple-element.41), channel_id=1, source_target_pairs={{0,4},{4,8},{8,12},{1,5},{5,9},{9,13},{2,6},{6,10},{10,14},{3,7},{... | collective-permute-start | bytes 1105928 | tf_op jit(solution)/shard_map/ppermute | solution.py:20
  31.3 1.3 %collective-permute-start.3 = (bf16[3,1,160,384]{3,2,1,0:T(8,128)(2,1)S(1)}, bf16[3,1,160,384]{3,2,1,0:T(8,128)(2,1)S(1)}, u32[]{:S(2)}, u32[]{:S(2)}) collective-permute-start(bf16[3,1,160,384]{3,2,1,0:T(8,128)(2,1)S(1)} %get-tuple-element.40), channel_id=1, source_target_pairs={{4,0},{8,4},{12,8},{5,1},{9,5},{13,9},{6,2},{10,6},{14,10},{7,3},{... | collective-permute-start | bytes 1105928 | tf_op jit(solution)/shard_map/ppermute | solution.py:21
  32.6 3.9 %fusion.53 = (bf16[1,1,3,384,384]{4,3,2,1,0:T(8,128)(2,1)S(1)}, bf16[1,1,3,384,384]{4,3,2,1,0:T(8,128)(2,1)S(1)}, bf16[1,1,3,384,384]{4,3,2,1,0:T(8,128)(2,1)S(1...) fusion(bf16[3,3,3,384,384]{4,3,2,1,0:T(8,128)(2,1)} %param.19), kind=kLoop, calls=%fused_computation.96 | loop fusion | bytes 15925248 | tf_op jit(solution)/shard_map/slice | solution.py:41
  36.6 1.5 %select_maximum_fusion = bf16[3,5,162,384]{3,2,1,0:T(8,128)(2,1)S(1)} fusion(bf16[3,1,160,384]{3,2,1,0:T(8,128)(2,1)S(1)} %collective-permute-done.3, bf16[3,1,160,384]{3,2,1,0:T(8,128)(2,1)S(1)} %collective-permute-done.2, bf16[1,3,160,384]{3,2,1,0:T(8,128)(2,1)S(1)} %fusion.43, bf16[1,3,160,384]{3,2,1,0:T(8,128)(2,1)S(1)} %collective-permute-done.1, ...), kind=kLoop, calls=%fused_computation.10 | loop fusion | flops 16796160 | bytes 3709440 | tf_op jit(solution)/shard_map/concatenate | solution.py:22
  38.1 1.1 %fusion.54 = (bf16[1,3,160,384]{3,2,1,0:T(8,128)(2,1)S(1)}, bf16[1,3,160,384]{3,2,1,0:T(8,128)(2,1)S(1)}, bf16[1,3,160,384]{3,2,1,0:T(8,128)(2,1)S(1)}, bf16[1,3...) fusion(bf16[3,5,162,384]{3,2,1,0:T(8,128)(2,1)S(1)} %select_max, ...), kind=kLoop, calls=%fused_computation.97 | loop fusion | bytes 13271040 | tf_op jit(solution)/shard_map/slice | solution.py:38
  39.3 1.3 %fusion.26 = (bf16[1,3,160,1152]{3,2,1,0:T(8,128)(2,1)S(1)}, bf16[1,3,160,1152]{3,2,1,0:T(8,128)(2,1)S(1)}, bf16[1,3,160,1152]{3,2,1,0:T(8,128)(2,1)S(1)}) fusion(bf16[3,1,160,384]{3,2,1,0:T(8,128)(2,1)S(1)} %collective-permute-done.2, bf16[1,3,160,384]{3,2,1,0:T(8,128)(2,1)S(1)} %fusion.43, bf16[1,3,160,384]{3,2,1,0:T(8,128)(2,1)S(1)} %collective-permute-done.1, ...), kind=kLoop, calls=%fused_computation.41 | loop fusion | flops 19906560 | bytes 7004160 | tf_op jit(solution)/shard_map/concatenate | solution.py:37
  40.5 0.8 fusion.55
  43.7 0.8 convolution_add_fusion.8
  45.3 0.8 convolution_add_fusion.6
  46.8 0.8 convolution_add_fusion.4
  47.6 0.8 convolution_add_fusion.3
  48.8 0.9 fusion.47
  49.8 1.4 %fusion.14 = bf16[480,384]{1,0:T(8,128)(2,1)S(1)} fusion(bf16[480,384]{1,0:T(8,128)(2,1)} %bitcast.75, bf16[384,384]{1,0:T(8,128)(2,1)S(1)} %copy-done.7, f32[384]{0:T(512)S(1)} %copy-done.10), kind=kOutput, calls=%fused_computation.31 | convolution fusion | flops 141926400 | bytes 1033728 | tf_op jit(solution)/shard_map/dot_general | solution.py:92
  51.2 32.2 %all-gather.2.cloned.1.call-done = bf16[1,12,160,384]{3,2,0,1:T(8,128)(2,1)} async-done(((bf16[1,3,160,384]{3,2,0,1:T(8,128)(2,1)}), bf16[1,12,160,384]{3,2,0,1:T(8,128)(2,1)}) %all-gather.2.cloned.1.call-update) | async-done | bytes 1474576 | tf_op jit(solution)/shard_map/all_gather | solution.py:100
  83.4 5.3 %multiply_reduce_fusion = (f32[480]{0:T(512)S(1)}, f32[480,1920]{1,0:T(8,128)}) fusion(bf16[480,384]{1,0:T(8,128)(2,1)S(1)} %fusion.14, bf16[1920,384]{1,0:T(8,128)(2,1)} %bitcast.79, bf16[384,384]{1,0:T(8,128)(2,1)S(1)} %copy-done), kind=kOutput, calls=%fused_computation.4 | convolution fusion | flops 1276599808 | bytes 5826432 | tf_op jit(solution)/shard_map/fqc,fkc->fqk/dot_general | solution.py:49
  88.7 2.2 %fusion.3 = bf16[1920,384]{1,0:T(8,128)(2,1)} fusion(bf16[1920,384]{1,0:T(8,128)(2,1)S(1)} %bitcast.80, bf16[384,384]{1,0:T(8,128)(2,1)S(1)} %copy-done.8, f32[384]{0:T(512)S(1)} %copy-done.11), kind=kOutput, calls=%fused_computation.9 | convolution fusion | flops 567705600 | bytes 3245568 | tf_op jit(solution)/shard_map/dot_general | solution.py:103
  92.4 3.5 %convolution_add_fusion.1 = f32[480,384]{1,0:T(8,128)S(1)} fusion(bf16[384,384]{1,0:T(8,128)(2,1)S(1)} %copy-done.9, bf16[1920,384]{1,0:T(8,128)(2,1)S(1)} %copy-done.13, f32[480,1920]{1,0:T(8,128)} %get-tuple-element.43, f32[480]{0:T(512)S(1)} %broadcast_maximum_fusion, f32[384]{0:T(512)S(1)} %copy-done.12, f32[480]{0:T(512)S(1)} %fusion.1), kind=kOutput, calls=%fused_computation.21 | convolution fusion | flops 852664320 | bytes 6198528 | tf_op jit(solution)/shard_map/dot_general | solution.py:107
  96.0 0.8 fusion.49
  (45 shorter events, 6.0 us)
Async XLA Ops:
  6.5 76.8 %copy-start = (bf16[384,384]{1,0:T(8,128)(2,1)S(1)}, bf16[384,384]{1,0:T(8,128)(2,1)}, u32[]{:S(2)}) copy-start(bf16[384,384]{1,0:T(8,128)(2,1)} %param.25) | copy-start | bytes 884740
  6.5 76.8 %all-gather.2.cloned.1.call-start = ((), (), s32[]{:S(2)}) async-start(), calls=%async_computation | async-start | bytes 1843200 | tf_op jit(solution)/shard_map/all_gather | solution.py:100
  9.1 13.9 %collective-permute-start.1 = (bf16[1,3,160,384]{3,2,1,0:T(8,128)(2,1)S(1)}, bf16[1,3,160,384]{3,2,1,0:T(8,128)(2,1)S(1)}, u32[]{:S(2)}, u32[]{:S(2)}) collective-permute-start(bf16[1,3,160,384]{3,2,1,0:T(8,128)(2,1)S(1)} %fusion.43), channel_id=1, source_target_pairs={{0,1},{1,2},{2,3},{4,5},{5,6},{6,7},{8,9},{9,10},{10,11},{12,13},{... | collective-permute-start | bytes 1105928 | tf_op jit(solution)/shard_map/ppermute | solution.py:10
  14.1 15.8 %collective-permute-start = (bf16[1,3,160,384]{3,2,1,0:T(8,128)(2,1)S(1)}, bf16[1,3,160,384]{3,2,1,0:T(8,128)(2,1)S(1)}, u32[]{:S(2)}, u32[]{:S(2)}) collective-permute-start(bf16[1,3,160,384]{3,2,1,0:T(8,128)(2,1)S(1)} %fusion.43), channel_id=1, source_target_pairs={{0,2},{1,3},{4,6},{5,7},{8,10},{9,11},{12,14},{13,15},{16,18},{17,... | collective-permute-start | bytes 1105928 | tf_op jit(solution)/shard_map/ppermute | solution.py:10
  29.9 6.6 %collective-permute-start.2 = (bf16[3,1,160,384]{3,2,1,0:T(8,128)(2,1)S(1)}, bf16[3,1,160,384]{3,2,1,0:T(8,128)(2,1)S(1)}, u32[]{:S(2)}, u32[]{:S(2)}) collective-permute-start(bf16[3,1,160,384]{3,2,1,0:T(8,128)(2,1)S(1)} %get-tuple-element.41), channel_id=1, source_target_pairs={{0,4},{4,8},{8,12},{1,5},{5,9},{9,13},{2,6},{6,10},{10,14},{3,7},{... | collective-permute-start | bytes 1105928 | tf_op jit(solution)/shard_map/ppermute | solution.py:20
  31.3 5.3 %collective-permute-start.3 = (bf16[3,1,160,384]{3,2,1,0:T(8,128)(2,1)S(1)}, bf16[3,1,160,384]{3,2,1,0:T(8,128)(2,1)S(1)}, u32[]{:S(2)}, u32[]{:S(2)}) collective-permute-start(bf16[3,1,160,384]{3,2,1,0:T(8,128)(2,1)S(1)} %get-tuple-element.40), channel_id=1, source_target_pairs={{4,0},{8,4},{12,8},{5,1},{9,5},{13,9},{6,2},{10,6},{14,10},{7,3},{... | collective-permute-start | bytes 1105928 | tf_op jit(solution)/shard_map/ppermute | solution.py:21
  47.6 1.0 copy-start.2
  47.6 1.0 copy-start.3
  47.6 1.2 %copy-start.4 = (f32[384]{0:T(512)S(1)}, f32[384]{0:T(512)}, u32[]{:S(2)}) copy-start(f32[384]{0:T(512)} %param.22) | copy-start | bytes 4612
  47.6 1.2 %copy-start.5 = (f32[384]{0:T(512)S(1)}, f32[384]{0:T(512)}, u32[]{:S(2)}) copy-start(f32[384]{0:T(512)} %param.21) | copy-start | bytes 4612
  48.4 1.4 %copy-start.7 = (bf16[384,384]{1,0:T(8,128)(2,1)S(1)}, bf16[384,384]{1,0:T(8,128)(2,1)}, u32[]{:S(2)}) copy-start(bf16[384,384]{1,0:T(8,128)(2,1)} %param.23) | copy-start | bytes 884740
  48.4 1.4 %copy-start.10 = (f32[384]{0:T(512)S(1)}, f32[384]{0:T(512)}, u32[]{:S(2)}) copy-start(f32[384]{0:T(512)} %param.24) | copy-start | bytes 4612
  83.3 5.4 %copy-start.6 = (bf16[1,12,160,384]{3,2,0,1:T(8,128)(2,1)S(1)}, bf16[1,12,160,384]{3,2,0,1:T(8,128)(2,1)}, u32[]{:S(2)}) copy-start(bf16[1,12,160,384]{3,2,0,1:T(8,128)(2,1)} %all-gather.2.cloned.1.call-done) | copy-start | bytes 4423684
  83.3 5.4 %copy-start.8 = (bf16[384,384]{1,0:T(8,128)(2,1)S(1)}, bf16[384,384]{1,0:T(8,128)(2,1)}, u32[]{:S(2)}) copy-start(bf16[384,384]{1,0:T(8,128)(2,1)} %param.26) | copy-start | bytes 884740
  83.3 5.4 %copy-start.11 = (f32[384]{0:T(512)S(1)}, f32[384]{0:T(512)}, u32[]{:S(2)}) copy-start(f32[384]{0:T(512)} %param.27) | copy-start | bytes 4612
  88.7 2.2 %copy-start.1 = (f32[480,1920]{1,0:T(8,128)S(1)}, f32[480,1920]{1,0:T(8,128)}, u32[]{:S(2)}) copy-start(f32[480,1920]{1,0:T(8,128)} %get-tuple-element.43) | copy-start | bytes 11059204
  90.9 1.0 copy-start.9
  90.9 1.0 copy-start.12
  90.9 1.5 %copy-start.13 = (bf16[1920,384]{1,0:T(8,128)(2,1)S(1)}, bf16[1920,384]{1,0:T(8,128)(2,1)}, u32[]{:S(2)}) copy-start(bf16[1920,384]{1,0:T(8,128)(2,1)} %fusion.3) | copy-start | bytes 4423684
Sparse Core Ops, SparseCore 0:
  49.9 33.4 all-gather.1
where the time goes:
time: 104 us
  waiting for transfers between devices  43.5 us (42%)
  matrix products  19.3 us (19%)
  between operations  13.7 us (13%)
  starting transfers between devices  12.1 us (12%)
  other arithmetic  9.02 us (9%)
  local copies, waits for them, and re-layouts  6.02 us (6%)
    all_gather x1, waiting for transfers between devices, shards(): lax.all_gather(normed, 'space', axis=1, tiled=True)  32.2 us
    ppermute x2, waiting for transfers between devices, from_behind(): lax.ppermute(value, axis, [(source, source + steps) for source in range(l...  11.2 us
    ppermute x2, starting transfers between devices, from_behind(): lax.ppermute(value, axis, [(source, source + steps) for source in range(l...  9.48 us
    dot_general x9, matrix products, causal_conv(): jnp.dot(joined, kernel, preferred_element_type=jnp.float32)  6.87 us
    dot_general x1, matrix products, absorb(): jnp.einsum('fqc,fkc->fqk', queries, key_rows, preferred_element_type=jnp....  5.34 us
    slice x1, local copies, waits for them, and re-layouts, causal_conv(): kernel = conv_weight[tap_t, tap_y].reshape(3 * channels, channels)  3.94 us
    dot_general x1, matrix products, shards(): jnp.dot(attended, out_weight, preferred_element_type=jnp.float32) + out_bias  3.54 us
    dot_general x1, matrix products, shards(): jnp.dot(source, value_weight, preferred_element_type=jnp.float32)  2.19 us
  transfers between devices with their start and end apart: 5, of which 4 were waited for; matrix products, arithmetic and copies ran while one was open for 5% of the time, Pallas kernels for 0%

commit v1 on v0

--- a/solution.py
+++ b/solution.py
@@ -1,7 +1,259 @@
+import functools
+
 import jax
 import jax.numpy as jnp
 from jax import lax
+from jax.experimental import pallas as pl
+from jax.experimental.pallas import tpu as pltpu
 from jax.sharding import PartitionSpec as P
+
+LOG2_E = 1.4426950408889634
+VMEM = pltpu.VMEM
+
+
+def ring(count, step):
+    return [(i, (i + step) % count) for i in range(count)]
+
+
+def pairs(count):
+    return [(i, i ^ 1) for i in range(count)]
+
+
+def edges_of(field):
+    bands = lax.axis_size("space")
+    rows = field.shape[1]
+    above = lax.ppermute(field[:, rows - 1 :], "space", ring(bands, 1))
+    below = lax.ppermute(field[:, :1], "space", ring(bands, -1))
+    return above, below
+
+
+def rms_scaled(wide, gain, bias):
+    mean_square = jnp.mean(wide * wide, axis=-1, keepdims=True)
+    return wide * lax.rsqrt(mean_square + 1e-06) * gain + bias
+
+
+def fill_row(taps, at, cells, keep, gain, bias):
+    columns, channels = cells.shape
+    wide = rms_scaled(cells.astype(jnp.float32), gain, bias)
+    active = wide / (1.0 + jnp.exp(-wide))
+    column = lax.broadcasted_iota(jnp.int32, (columns, channels), 0)
+    if keep is not None:
+        active = jnp.where(keep, active, 0.0)
+    left = jnp.where(column == 0, 0.0, pltpu.roll(active, 1, 0))
+    right = jnp.where(column == columns - 1, 0.0, pltpu.roll(active, columns - 1, 0))
+    span = pl.ds(at * columns, columns)
+    taps[span, 0:channels] = left.astype(jnp.bfloat16)
+    taps[span, channels : 2 * channels] = active.astype(jnp.bfloat16)
+    taps[span, 2 * channels : 3 * channels] = right.astype(jnp.bfloat16)
+
+
+def conv_body(first, last, columns, *refs):
+    (flags, field, above, below, gain, bias, kernel, start), refs = refs[:8], refs[8:]
+    if first:
+        conv_bias, total, taps = refs
+    elif last:
+        attn_gain, attn_bias, query_w, query_b, key_w, mixed, normed, queries, taps, total = refs
+    else:
+        total, taps = refs
+    tap = pl.program_id(0)
+    cells = field.shape[0]
+    rows = cells // columns
+
+    @pl.when(tap == 0)
+    def _():
+        here, over, under = (flags[0, i] > 0 for i in range(3))
+        for row in range(rows):
+            fill_row(taps, row + 1, field[row * columns : (row + 1) * columns], here, gain[...], bias[...])
+        fill_row(taps, 0, above[...], over, gain[...], bias[...])
+        fill_row(taps, rows + 1, below[...], under, gain[...], bias[...])
+        if first:
+            total[...] = start[...].astype(jnp.float32) + conv_bias[...]
+        else:
+            total[...] = start[...]
+
+    window = taps[pl.ds(pl.multiple_of(tap * columns, 16), cells), :]
+    total[...] += jnp.dot(window, kernel[...], preferred_element_type=jnp.float32)
+
+    if last:
+
+        @pl.when(tap == 2)
+        def _():
+            channels = field.shape[1]
+            rounded = total[...].astype(jnp.bfloat16)
+            mixed[...] = rounded
+            norm = rms_scaled(rounded.astype(jnp.float32), attn_gain[...], attn_bias[...])
+            norm = norm.astype(jnp.bfloat16)
+            normed[...] = norm
+            query = jnp.dot(norm, query_w[...], preferred_element_type=jnp.float32) + query_b[...]
+            query = query.astype(jnp.bfloat16)
+            folded = lax.dot_general(
+                query, key_w[...], (((1,), (1,)), ((), ())), preferred_element_type=jnp.float32
+            )
+            queries[...] = (folded * (LOG2_E * float(channels) ** -0.5)).astype(jnp.bfloat16)
+
+
+def whole(shape):
+    return pl.BlockSpec(shape, lambda i: (0,) * len(shape))
+
+
+def conv_step(which, flags, field, above, below, gain, bias, kernels, start, extra=()):
+    _, rows, columns, channels = field.shape
+    cells = rows * columns
+    first, last = which == 0, which == 2
+    flat = (cells, channels)
+    taken = kernels.shape[0] // 3 - 1 - which
+    scratch = [pltpu.VMEM(((rows + 2) * columns, 3 * channels), jnp.bfloat16)]
+    if last:
+        out_shape = [jax.ShapeDtypeStruct(flat, jnp.bfloat16)] * 3
+        out_specs = [whole(flat)] * 3
+        scratch.append(pltpu.VMEM(flat, jnp.float32))
+    else:
+        out_shape = jax.ShapeDtypeStruct(flat, jnp.float32)
+        out_specs = whole(flat)
+    arrays = [field.reshape(flat), above.reshape(columns, channels), below.reshape(columns, channels)]
+    arrays += [gain, bias]
+    specs = [whole(a.shape) for a in arrays]
+    specs.append(pl.BlockSpec((None, 3 * channels, channels), lambda i: (3 * taken + i, 0, 0)))
+    tail = [start.reshape(flat), *extra]
+    specs += [whole(a.shape) for a in tail]
+    return pl.pallas_call(
+        functools.partial(conv_body, first, last, columns),
+        grid=(3,),
+        in_specs=[pl.BlockSpec(memory_space=pltpu.SMEM), *specs],
+        out_specs=out_specs,
+        out_shape=out_shape,
+        scratch_shapes=scratch,
+        name=("conv_own", "conv_prev", "conv_last")[which],
+    )(flags, *arrays, kernels, *tail)
+
+
+def attn_body(count, resumed, last, *refs):
+    queries, refs = refs[0], refs[1:]
+    blocks, refs = refs[:count], refs[count:]
+    if resumed:
+        (numer_in, denom_in, high_in), refs = refs[:3], refs[3:]
+    if last:
+        value_w, value_b, out_w, out_b, mixed, result = refs
+    else:
+        numer_out, denom_out, high_out = refs
+    cells, channels = queries.shape
+    tile = 160 if cells % 160 == 0 else cells
+    for part in range(cells // tile):
+        span = slice(part * tile, (part + 1) * tile)
+        query = queries[span]
+        if resumed:
+            numer, denom, high = numer_in[span], denom_in[span, 0:1], high_in[span, 0:1]
+        else:
+            numer = denom = high = None
+        for block in blocks:
+            keys = block[...]
+            scores = lax.dot_general(
+                query, keys, (((1,), (1,)), ((), ())), preferred_element_type=jnp.float32
+            )
+            top = jnp.max(scores, axis=-1, keepdims=True)
+            fresh = top if high is None else jnp.maximum(high, top)
+            expd = jnp.exp2(scores - fresh)
+            added = jnp.dot(expd.astype(jnp.bfloat16), keys, preferred_element_type=jnp.float32)
+            count_up = jnp.sum(expd, axis=-1, keepdims=True)
+            if high is None:
+                numer, denom = added, count_up
+            else:
+                decay = jnp.exp2(high - fresh)
+                numer, denom = numer * decay + added, denom * decay + count_up
+            high = fresh
+        if last:
+            pooled = (numer / denom).astype(jnp.bfloat16)
+            attended = jnp.dot(pooled, value_w[...], preferred_element_type=jnp.float32) + value_b[...]
+            attended = attended.astype(jnp.bfloat16)
+            projected = jnp.dot(attended, out_w[...], preferred_element_type=jnp.float32) + out_b[...]
+            result[span] = (mixed[span].astype(jnp.float32) + projected).astype(jnp.bfloat16)
+        else:
+            numer_out[span] = numer
+            denom_out[span] = jnp.broadcast_to(denom, (tile, 128))
+            high_out[span] = jnp.broadcast_to(high, (tile, 128))
+
+
+def attn_step(name, queries, blocks, state, closing=None):
+    cells, channels = queries.shape
+    arrays = [queries, *blocks, *(state or ())]
+    if closing is not None:
+        arrays += closing
+        out_shape = jax.ShapeDtypeStruct((cells, channels), jnp.bfloat16)
+    else:
+        out_shape = [
+            jax.ShapeDtypeStruct((cells, channels), jnp.float32),
+            jax.ShapeDtypeStruct((cells, 128), jnp.float32),
+            jax.ShapeDtypeStruct((cells, 128), jnp.float32),
+        ]
+    vmem = pl.BlockSpec(memory_space=VMEM)
+    return pl.pallas_call(
+        functools.partial(attn_body, len(blocks), state is not None, closing is not None),
+        in_specs=[vmem] * len(arrays),
+        out_specs=vmem if closing is not None else [vmem] * 3,
+        out_shape=out_shape,
+        name=name,
+    )(*arrays)
+
+
+def single_frame(
+    block_input,
+    conv_input,
+    norm_gain,
+    norm_bias,
+    conv_weight,
+    conv_bias,
+    attn_gain,
+    attn_bias,
+    query_weight,
+    query_bias,
+    key_weight,
+    value_weight,
+    value_bias,
+    out_weight,
+    out_bias,
+):
+    _, rows, columns, channels = block_input.shape
+    bands, groups = lax.axis_size("space"), lax.axis_size("tm")
+    band, group = lax.axis_index("space"), lax.axis_index("tm")
+    line = lambda v: v.reshape(1, channels)
+    kernels = conv_weight.reshape(9, 3 * channels, channels)
+    gain, bias = line(norm_gain), line(norm_bias)
+
+    def flags(back):
+        here = group >= back
+        return jnp.stack([here, here & (band > 0), here & (band < bands - 1)]).astype(jnp.int32)[None]
+
+    frame = conv_input
+    prev = lax.ppermute(frame, "tm", ring(groups, 1))
+    above, below = edges_of(frame)
+    total = conv_step(0, flags(0), frame, above, below, gain, bias, kernels, block_input, [line(conv_bias)])
+    older = lax.ppermute(prev, "tm", ring(groups, 1))
+    above, below = edges_of(prev)
+    total = conv_step(1, flags(1), prev, above, below, gain, bias, kernels, total)
+    above, below = edges_of(older)
+    extra = [line(attn_gain), line(attn_bias), query_weight, line(query_bias), key_weight]
+    mixed, normed, queries = conv_step(
+        2, flags(2), older, above, below, gain, bias, kernels, total, extra
+    )
+    closing = [value_weight, line(value_bias), out_weight, line(out_bias), mixed]
+    chips = bands // 2
+    far = normed
+    state = None
+    far = [(i, (i + 2) % bands) for i in range(bands)]
+    crossing = normed
+    waves = []
+    for _ in range(chips - 1):
+        crossing = lax.ppermute(crossing, "space", far)
+        waves.append(crossing)
+    near = lax.ppermute(normed, "space", pairs(bands))
+    state = attn_step("attn_near", queries, [normed, near], state)
+    for i, wave in enumerate(waves):
+        beside = lax.ppermute(wave, "space", pairs(bands))
+        state = attn_step("attn_far", queries, [wave], state)
+        if i < len(waves) - 1:
+            state = attn_step("attn_beside", queries, [beside], state)
+    result = attn_step("attn_close", queries, [beside], state, closing)
+    return result.reshape(block_input.shape)
 
 
 def from_behind(value, axis, steps):
@@ -76,6 +328,24 @@
     out_bias,
 ):
     frame_count, row_count, columns, channels = block_input.shape
+    if frame_count == 1 and lax.axis_size("space") % 2 == 0 and lax.axis_size("space") > 2:
+        return single_frame(
+            block_input,
+            conv_input,
+            norm_gain,
+            norm_bias,
+            conv_weight,
+            conv_bias,
+            attn_gain,
+            attn_bias,
+            query_weight,
+            query_bias,
+            key_weight,
+            value_weight,
+            value_bias,
+            out_weight,
+            out_bias,
+        )
     field = conv_input.astype(jnp.float32)
     activated = jax.nn.silu(rms_norm(field, norm_gain, norm_bias)).astype(jnp.bfloat16)
     earlier = [from_behind(activated, "tm", offset) for offset in (1, 2)]

time: 104 us -> 85.3 us (0.82)
  Pallas kernels: 0 us -> 33.4 us
  matrix products: 19.3 us -> 0 us
  waiting for transfers between devices: 43.5 us -> 26.1 us
  between operations: 13.7 us -> 0.14 us
  local copies, waits for them, and re-layouts: 6.02 us -> 13.4 us
  other arithmetic: 9.02 us -> 1.94 us
  starting transfers between devices: 12.1 us -> 9.72 us
    pallas_call x0 -> x6, Pallas kernels: none -> 33.4 us  [the longest x3 19.1 us: conv_step(): pl.pallas_call(functools.partial(conv_body, first, last, columns), grid=(...]
    all_gather x1 -> x0, waiting for transfers between devices: 32.2 us -> none  [shards(): lax.all_gather(normed, 'space', axis=1, tiled=True)]
    dot_general x13 -> x0, matrix products: 19.3 us -> none  [the longest x9 6.87 us: causal_conv(): jnp.dot(joined, kernel, preferred_element_type=jnp.float32)]
    ppermute x4 -> x11, waiting for transfers between devices: 11.3 us -> 26.1 us  [the longest x1 10.8 us: single_frame(): prev = lax.ppermute(frame, 'tm', ring(groups, 1))]
    reshape x0 -> x8, local copies, waits for them, and re-layouts: none -> 8.73 us  [single_frame(): line = lambda v: v.reshape(1, channels)]
    slice x2 -> x3, local copies, waits for them, and re-layouts: 5.07 us -> 1.17 us  [edges_of(): below = lax.ppermute(field[:, :1], 'space', ring(bands, -1))]
    concatenate x6 -> x0, other arithmetic: 3.77 us -> none  [the longest x4 2.13 us: causal_conv(): jnp.concatenate([window[:, :, tap_x:tap_x + columns] for tap_x in range(3...]
    unnamed x28 -> x26, local copies, waits for them, and re-layouts: 0.95 us -> 3.53 us
  transfers between devices with their start and end apart: 5 -> 11, of which waited for: 4 -> 3; matrix products, arithmetic and copies ran while one was open for 5% -> 14% of each run, Pallas kernels for 0% -> 25%
where the time goes in v1:
time: 85.3 us; the launch traced here: 84.8 us
  Pallas kernels  33.4 us (39%)
  waiting for transfers between devices  26.1 us (31%)
  local copies, waits for them, and re-layouts  13.4 us (16%)
  starting transfers between devices  9.72 us (11%)
  other arithmetic  1.94 us (2%)
    pallas_call x3, Pallas kernels, conv_step(): pl.pallas_call(functools.partial(conv_body, first, last, columns), grid=(...  19.1 us
    pallas_call x3, Pallas kernels, attn_step(): pl.pallas_call(functools.partial(attn_body, len(blocks), state is not Non...  14.3 us
    ppermute x1, waiting for transfers between devices, single_frame(): prev = lax.ppermute(frame, 'tm', ring(groups, 1))  10.8 us
    ppermute x1, waiting for transfers between devices, single_frame(): crossing = lax.ppermute(crossing, 'space', far)  9.08 us
    reshape x8, local copies, waits for them, and re-layouts, single_frame(): line = lambda v: v.reshape(1, channels)  8.73 us
    ppermute x1, waiting for transfers between devices, single_frame(): older = lax.ppermute(prev, 'tm', ring(groups, 1))  6.18 us
    ppermute x3, starting transfers between devices, edges_of(): below = lax.ppermute(field[:, :1], 'space', ring(bands, -1))  5.18 us
    unnamed x26, local copies, waits for them, and re-layouts  3.53 us
  transfers between devices with their start and end apart: 11, of which 3 were waited for; matrix products, arithmetic and copies ran while one was open for 14% of the time, Pallas kernels for 25%

profile of v1, /device:TPU:0, one launch (start us, length us, event | category | flops | bytes accessed | tf_op | source)
XLA Modules:
  0.0 84.8 jit_solution(17766756088578006776)
XLA Ops:
  0.0 3.1 %collective-permute-start = (bf16[1,3,160,384]{3,2,1,0:T(8,128)(2,1)}, bf16[1,3,160,384]{3,2,1,0:T(8,128)(2,1)S(1)}, u32[]{:S(2)}, u32[]{:S(2)}) collective-permute-start(bf16[1,3,160,384]{3,2,1,0:T(8,128)(2,1)} %param.16), channel_id=1, source_target_pairs={{0,1},{1,2},{2,3},{3,0},{4,5},{5,6},{6,7},{7,4},{8,9},{9,10},{10,1... | collective-permute-start | bytes 1105928 | tf_op jit(solution)/shard_map/ppermute | solution.py:227
  3.1 10.8 %collective-permute-done = bf16[1,3,160,384]{3,2,1,0:T(8,128)(2,1)S(1)} collective-permute-done((bf16[1,3,160,384]{3,2,1,0:T(8,128)(2,1)}, bf16[1,3,160,384]{3,2,1,0:T(8,128)(2,1)S(1)}, u32[]{:S(2)}, u32[]{:S(2)}) %collective-permute-start) | collective-permute-done | bytes 368672 | tf_op jit(solution)/shard_map/ppermute | solution.py:227
  13.9 1.1 %fusion = (bf16[1,1,160,384]{3,2,1,0:T(8,128)(2,1)S(1)}, bf16[1,1,160,384]{3,2,1,0:T(8,128)(2,1)S(1)}) fusion(bf16[1,3,160,384]{3,2,1,0:T(8,128)(2,1)} %param.16), kind=kLoop, calls=%fused_computation.3 | loop fusion | bytes 491520 | tf_op jit(solution)/shard_map/slice | solution.py:26
  15.1 1.7 %collective-permute-start.7 = (bf16[1,1,160,384]{3,2,1,0:T(8,128)(2,1)S(1)}, bf16[1,1,160,384]{3,2,1,0:T(8,128)(2,1)S(1)}, u32[]{:S(2)}, u32[]{:S(2)}) collective-permute-start(bf16[1,1,160,384]{3,2,1,0:T(8,128)(2,1)S(1)} %get-tuple-element.23), channel_id=1, source_target_pairs={{0,12},{4,0},{8,4},{12,8},{1,13},{5,1},{9,5},{13,9},{2,14},{6,2},{... | collective-permute-start | bytes 368648 | tf_op jit(solution)/shard_map/ppermute | solution.py:26
  17.5 1.7 %collective-permute-start.5 = (bf16[1,1,160,384]{3,2,1,0:T(8,128)(2,1)S(1)}, bf16[1,1,160,384]{3,2,1,0:T(8,128)(2,1)S(1)}, u32[]{:S(2)}, u32[]{:S(2)}) collective-permute-start(bf16[1,1,160,384]{3,2,1,0:T(8,128)(2,1)S(1)} %get-tuple-element.25), channel_id=1, source_target_pairs={{0,12},{4,0},{8,4},{12,8},{1,13},{5,1},{9,5},{13,9},{2,14},{6,2},{... | collective-permute-start | bytes 368648 | tf_op jit(solution)/shard_map/ppermute | solution.py:26
  19.2 6.2 %collective-permute-done.1 = bf16[1,3,160,384]{3,2,1,0:T(8,128)(2,1)S(1)} collective-permute-done((bf16[1,3,160,384]{3,2,1,0:T(8,128)(2,1)S(1)}, bf16[1,3,160,384]{3,2,1,0:T(8,128)(2,1)S(1)}, u32[]{:S(2)}, u32[]{:S(2)}) %collective-permute-start.1) | collective-permute-done | bytes 368672 | tf_op jit(solution)/shard_map/ppermute | solution.py:230
  25.5 1.7 %collective-permute-start.3 = (bf16[1,1,160,384]{3,2,1,0:T(8,128)(2,1)S(1)}, bf16[1,1,160,384]{3,2,1,0:T(8,128)(2,1)S(1)}, u32[]{:S(2)}, u32[]{:S(2)}) collective-permute-start(bf16[1,1,160,384]{3,2,1,0:T(8,128)(2,1)S(1)} %get-tuple-element.27), channel_id=1, source_target_pairs={{0,12},{4,0},{8,4},{12,8},{1,13},{5,1},{9,5},{13,9},{2,14},{6,2},{... | collective-permute-start | bytes 368648 | tf_op jit(solution)/shard_map/ppermute | solution.py:26
  27.9 1.3 %reshape.198.refs_4_ = f32[1,384]{1,0:T(1,128)} reshape(f32[384]{0:T(512)} %param.17) | data formatting | bytes 3072 | tf_op jit(solution)/shard_map/reshape | solution.py:218
  29.2 1.3 %reshape.199.refs_5_ = f32[1,384]{1,0:T(1,128)} reshape(f32[384]{0:T(512)} %param.18) | data formatting | bytes 3072 | tf_op jit(solution)/shard_map/reshape | solution.py:218
  30.5 1.3 %reshape.208.refs_8_ = f32[1,384]{1,0:T(1,128)} reshape(f32[384]{0:T(512)} %param.20) | data formatting | bytes 3072 | tf_op jit(solution)/shard_map/reshape | solution.py:218
  31.7 1.3 %reshape.209.refs_8_ = f32[1,384]{1,0:T(1,128)} reshape(f32[384]{0:T(512)} %param.21) | data formatting | bytes 3072 | tf_op jit(solution)/shard_map/reshape | solution.py:218
  33.0 1.3 %reshape.210.refs_9_ = f32[1,384]{1,0:T(1,128)} reshape(f32[384]{0:T(512)} %param.22) | data formatting | bytes 3072 | tf_op jit(solution)/shard_map/reshape | solution.py:218
  34.2 1.2 %reshape.211.refs_11_ = f32[1,384]{1,0:T(1,128)} reshape(f32[384]{0:T(512)} %param.24) | data formatting | bytes 3072 | tf_op jit(solution)/shard_map/reshape | solution.py:218
  35.5 0.7 add_convert_fusion.refs_0_
  36.8 6.0 %conv_own.1.refs_7_ = f32[480,384]{1,0:T(8,128)} custom-call(s32[1,3]{1,0:T(1,128)} %add_convert_fusion.2.refs_0_, bf16[480,384]{1,0:T(8,128)(2,1)} %bitcast.24, bf16[160,384]{1,0:T(8,128)(2,1)} %bitcast.28, bf16[160,384]{1,0:T(8,128)(2,1)} %bitcast.29, f32[1,384]{1,0:T(1,128)} %reshape.198.refs_4_, f32[1,384]{1,0:T(1,128)} %reshape.199.refs_5_, ...), custom_call_target="tpu_custom_call" | custom-call | tf_op jit(solution)/shard_map/conv_own/pallas_call | solution.py:119
  43.5 6.1 %conv_prev.1.refs_7_ = f32[480,384]{1,0:T(8,128)} custom-call(s32[1,3]{1,0:T(1,128)} %add_convert_fusion.1.refs_0_, bf16[480,384]{1,0:T(8,128)(2,1)} %bitcast.26, bf16[160,384]{1,0:T(8,128)(2,1)} %bitcast.31, bf16[160,384]{1,0:T(8,128)(2,1)} %bitcast.32, f32[1,384]{1,0:T(1,128)} %reshape.198.refs_4_, f32[1,384]{1,0:T(1,128)} %reshape.199.refs_5_, ...), custom_call_target="tpu_custom_call" | custom-call | tf_op jit(solution)/shard_map/conv_prev/pallas_call | solution.py:119
  50.3 7.1 %conv_last.1 = (bf16[480,384]{1,0:T(8,128)(2,1)}, bf16[480,384]{1,0:T(8,128)(2,1)}, bf16[480,384]{1,0:T(8,128)(2,1)}) custom-call(s32[1,3]{1,0:T(1,128)} %add_convert_fusion.refs_0_, bf16[480,384]{1,0:T(8,128)(2,1)} %bitcast.25, bf16[160,384]{1,0:T(8,128)(2,1)} %bitcast.30, bf16[160,384]{1,0:T(8,128)(2,1)} %bitcast.33, f32[1,384]{1,0:T(1,128)} %reshape.198.refs_4_, ...), custom_call_target="tpu_custom_call" | custom-call | tf_op jit(solution)/shard_map/conv_last/pallas_call | solution.py:119
  57.4 1.3 %collective-permute-start.8 = (bf16[480,384]{1,0:T(8,128)(2,1)}, bf16[480,384]{1,0:T(8,128)(2,1)S(1)}, u32[]{:S(2)}, u32[]{:S(2)}) collective-permute-start(bf16[480,384]{1,0:T(8,128)(2,1)} %get-tuple-element.15.refs_1_), channel_id=1, source_target_pairs={{0,8},{4,12},{8,0},{12,4},{1,9},{5,13},{9,1},{13,5},{2,10},{6,14},... | collective-permute-start | bytes 1105928 | tf_op jit(solution)/shard_map/ppermute | solution.py:246
  58.7 9.1 %collective-permute-done.8.refs_1_ = bf16[480,384]{1,0:T(8,128)(2,1)S(1)} collective-permute-done((bf16[480,384]{1,0:T(8,128)(2,1)}, bf16[480,384]{1,0:T(8,128)(2,1)S(1)}, u32[]{:S(2)}, u32[]{:S(2)}) %collective-permute-start.8) | collective-permute-done | bytes 368672 | tf_op jit(solution)/shard_map/ppermute | solution.py:246
  68.9 0.7 copy-done.3
  69.7 4.9 %attn_near.1 = (f32[480,384]{1,0:T(8,128)}, f32[480,128]{1,0:T(8,128)}, f32[480,128]{1,0:T(8,128)}) custom-call(bf16[480,384]{1,0:T(8,128)(2,1)} %get-tuple-element.14.refs_0_, bf16[480,384]{1,0:T(8,128)(2,1)} %get-tuple-element.15.refs_1_, bf16[480,384]{1,0:T(8,128)(2,1)} %copy-done.3), custom_call_target="tpu_custom_call" | custom-call | tf_op jit(solution)/shard_map/attn_near/pallas_call | solution.py:189
  74.6 4.2 %attn_far.1 = (f32[480,384]{1,0:T(8,128)}, f32[480,128]{1,0:T(8,128)}, f32[480,128]{1,0:T(8,128)}) custom-call(bf16[480,384]{1,0:T(8,128)(2,1)} %get-tuple-element.14.refs_0_, bf16[480,384]{1,0:T(8,128)(2,1)} %copy-done.4, f32[480,384]{1,0:T(8,128)} %get-tuple-element.16.refs_2_, f32[480,128]{1,0:T(8,128)} %get-tuple-element.17.refs_3_, ...), custom_call_target="tpu_custom_call" | custom-call | tf_op jit(solution)/shard_map/attn_far/pallas_call | solution.py:189
  78.7 0.8 copy-done.2
  79.5 5.3 %attn_close.1 = bf16[480,384]{1,0:T(8,128)(2,1)} custom-call(bf16[480,384]{1,0:T(8,128)(2,1)} %get-tuple-element.14.refs_0_, bf16[480,384]{1,0:T(8,128)(2,1)} %copy-done.2, f32[480,384]{1,0:T(8,128)} %get-tuple-element.19.refs_2_, f32[480,128]{1,0:T(8,128)} %get-tuple-element.20.refs_3_, f32[480,128]{1,0:T(8,128)} %get-tuple-element.21.refs_4_, ...), custom_call_target="tpu_custom_call" | custom-call | tf_op jit(solution)/shard_map/attn_close/pallas_call | solution.py:189
  (44 shorter events, 4.7 us)
Async XLA Ops:
  0.0 13.9 %collective-permute-start = (bf16[1,3,160,384]{3,2,1,0:T(8,128)(2,1)}, bf16[1,3,160,384]{3,2,1,0:T(8,128)(2,1)S(1)}, u32[]{:S(2)}, u32[]{:S(2)}) collective-permute-start(bf16[1,3,160,384]{3,2,1,0:T(8,128)(2,1)} %param.16), channel_id=1, source_target_pairs={{0,1},{1,2},{2,3},{3,0},{4,5},{5,6},{6,7},{7,4},{8,9},{9,10},{10,1... | collective-permute-start | bytes 1105928 | tf_op jit(solution)/shard_map/ppermute | solution.py:227
  13.9 28.9 %copy-start.1 = (bf16[1,3,160,384]{3,2,1,0:T(8,128)(2,1)}, bf16[1,3,160,384]{3,2,1,0:T(8,128)(2,1)S(1)}, u32[]{:S(2)}) copy-start(bf16[1,3,160,384]{3,2,1,0:T(8,128)(2,1)S(1)} %collective-permute-done) | copy-start | bytes 1105924
  13.9 11.6 %collective-permute-start.1 = (bf16[1,3,160,384]{3,2,1,0:T(8,128)(2,1)S(1)}, bf16[1,3,160,384]{3,2,1,0:T(8,128)(2,1)S(1)}, u32[]{:S(2)}, u32[]{:S(2)}) collective-permute-start(bf16[1,3,160,384]{3,2,1,0:T(8,128)(2,1)S(1)} %collective-permute-done), channel_id=1, source_target_pairs={{0,1},{1,2},{2,3},{3,0},{4,5},{5,6},{6,7},{7,4},{8,9},{9,10},{10,1... | collective-permute-start | bytes 1105928 | tf_op jit(solution)/shard_map/ppermute | solution.py:230
  15.0 10.5 %collective-permute-start.6 = (bf16[1,1,160,384]{3,2,1,0:T(8,128)(2,1)S(1)}, bf16[1,1,160,384]{3,2,1,0:T(8,128)(2,1)S(1)}, u32[]{:S(2)}, u32[]{:S(2)}) collective-permute-start(bf16[1,1,160,384]{3,2,1,0:T(8,128)(2,1)S(1)} %get-tuple-element.24), channel_id=1, source_target_pairs={{0,4},{4,8},{8,12},{12,0},{1,5},{5,9},{9,13},{13,1},{2,6},{6,10},{... | collective-permute-start | bytes 368648 | tf_op jit(solution)/shard_map/ppermute | solution.py:25
  15.1 21.1 %collective-permute-start.7 = (bf16[1,1,160,384]{3,2,1,0:T(8,128)(2,1)S(1)}, bf16[1,1,160,384]{3,2,1,0:T(8,128)(2,1)S(1)}, u32[]{:S(2)}, u32[]{:S(2)}) collective-permute-start(bf16[1,1,160,384]{3,2,1,0:T(8,128)(2,1)S(1)} %get-tuple-element.23), channel_id=1, source_target_pairs={{0,12},{4,0},{8,4},{12,8},{1,13},{5,1},{9,5},{13,9},{2,14},{6,2},{... | collective-permute-start | bytes 368648 | tf_op jit(solution)/shard_map/ppermute | solution.py:26
  17.4 25.3 %collective-permute-start.4 = (bf16[1,1,160,384]{3,2,1,0:T(8,128)(2,1)S(1)}, bf16[1,1,160,384]{3,2,1,0:T(8,128)(2,1)S(1)}, u32[]{:S(2)}, u32[]{:S(2)}) collective-permute-start(bf16[1,1,160,384]{3,2,1,0:T(8,128)(2,1)S(1)} %get-tuple-element.26), channel_id=1, source_target_pairs={{0,4},{4,8},{8,12},{12,0},{1,5},{5,9},{9,13},{13,1},{2,6},{6,10},{... | collective-permute-start | bytes 368648 | tf_op jit(solution)/shard_map/ppermute | solution.py:25
  17.5 25.3 %collective-permute-start.5 = (bf16[1,1,160,384]{3,2,1,0:T(8,128)(2,1)S(1)}, bf16[1,1,160,384]{3,2,1,0:T(8,128)(2,1)S(1)}, u32[]{:S(2)}, u32[]{:S(2)}) collective-permute-start(bf16[1,1,160,384]{3,2,1,0:T(8,128)(2,1)S(1)} %get-tuple-element.25), channel_id=1, source_target_pairs={{0,12},{4,0},{8,4},{12,8},{1,13},{5,1},{9,5},{13,9},{2,14},{6,2},{... | collective-permute-start | bytes 368648 | tf_op jit(solution)/shard_map/ppermute | solution.py:26
  25.4 24.1 %copy-start = (bf16[1,3,160,384]{3,2,1,0:T(8,128)(2,1)}, bf16[1,3,160,384]{3,2,1,0:T(8,128)(2,1)S(1)}, u32[]{:S(2)}) copy-start(bf16[1,3,160,384]{3,2,1,0:T(8,128)(2,1)S(1)} %collective-permute-done.1) | copy-start | bytes 1105924
  25.5 24.1 %collective-permute-start.2 = (bf16[1,1,160,384]{3,2,1,0:T(8,128)(2,1)S(1)}, bf16[1,1,160,384]{3,2,1,0:T(8,128)(2,1)S(1)}, u32[]{:S(2)}, u32[]{:S(2)}) collective-permute-start(bf16[1,1,160,384]{3,2,1,0:T(8,128)(2,1)S(1)} %get-tuple-element.28), channel_id=1, source_target_pairs={{0,4},{4,8},{8,12},{12,0},{1,5},{5,9},{9,13},{13,1},{2,6},{6,10},{... | collective-permute-start | bytes 368648 | tf_op jit(solution)/shard_map/ppermute | solution.py:25
  25.5 10.6 %copy-start.5 = (bf16[1,1,160,384]{3,2,1,0:T(8,128)(2,1)}, bf16[1,1,160,384]{3,2,1,0:T(8,128)(2,1)S(1)}, u32[]{:S(2)}) copy-start(bf16[1,1,160,384]{3,2,1,0:T(8,128)(2,1)S(1)} %collective-permute-done.6) | copy-start | bytes 368644
  25.5 24.0 %collective-permute-start.3 = (bf16[1,1,160,384]{3,2,1,0:T(8,128)(2,1)S(1)}, bf16[1,1,160,384]{3,2,1,0:T(8,128)(2,1)S(1)}, u32[]{:S(2)}, u32[]{:S(2)}) collective-permute-start(bf16[1,1,160,384]{3,2,1,0:T(8,128)(2,1)S(1)} %get-tuple-element.27), channel_id=1, source_target_pairs={{0,12},{4,0},{8,4},{12,8},{1,13},{5,1},{9,5},{13,9},{2,14},{6,2},{... | collective-permute-start | bytes 368648 | tf_op jit(solution)/shard_map/ppermute | solution.py:26
  36.1 0.6 copy-start.6
  42.8 0.6 copy-start.8
  42.8 0.7 copy-start.9
  43.5 24.3 %copy-start.11 = (f32[384]{0:T(512)S(1)}, f32[384]{0:T(512)}, u32[]{:S(2)}) copy-start(f32[384]{0:T(512)} %param.27) | copy-start | bytes 4612
  43.5 24.9 %copy-start.12 = (f32[384]{0:T(512)S(1)}, f32[384]{0:T(512)}, u32[]{:S(2)}) copy-start(f32[384]{0:T(512)} %param.29) | copy-start | bytes 4612
  49.6 0.7 copy-start.7
  49.6 0.7 copy-start.10
  57.4 10.4 %collective-permute-start.8 = (bf16[480,384]{1,0:T(8,128)(2,1)}, bf16[480,384]{1,0:T(8,128)(2,1)S(1)}, u32[]{:S(2)}, u32[]{:S(2)}) collective-permute-start(bf16[480,384]{1,0:T(8,128)(2,1)} %get-tuple-element.15.refs_1_), channel_id=1, source_target_pairs={{0,8},{4,12},{8,0},{12,4},{1,9},{5,13},{9,1},{13,5},{2,10},{6,14},... | collective-permute-start | bytes 1105928 | tf_op jit(solution)/shard_map/ppermute | solution.py:246
  58.7 10.3 %collective-permute-start.10 = (bf16[480,384]{1,0:T(8,128)(2,1)}, bf16[480,384]{1,0:T(8,128)(2,1)S(1)}, u32[]{:S(2)}, u32[]{:S(2)}) collective-permute-start(bf16[480,384]{1,0:T(8,128)(2,1)} %get-tuple-element.15.refs_1_), channel_id=1, source_target_pairs={{0,4},{4,0},{8,12},{12,8},{1,5},{5,1},{9,13},{13,9},{2,6},{6,2},{1... | collective-permute-start | bytes 1105928 | tf_op jit(solution)/shard_map/ppermute | solution.py:248
  67.7 6.8 %copy-start.4 = (bf16[480,384]{1,0:T(8,128)(2,1)}, bf16[480,384]{1,0:T(8,128)(2,1)S(1)}, u32[]{:S(2)}) copy-start(bf16[480,384]{1,0:T(8,128)(2,1)S(1)} %collective-permute-done.8.refs_1_) | copy-start | bytes 1105924
  67.7 11.0 %collective-permute-start.9 = (bf16[480,384]{1,0:T(8,128)(2,1)S(1)}, bf16[480,384]{1,0:T(8,128)(2,1)S(1)}, u32[]{:S(2)}, u32[]{:S(2)}) collective-permute-start(bf16[480,384]{1,0:T(8,128)(2,1)S(1)} %collective-permute-done.8.refs_1_), channel_id=1, source_target_pairs={{0,4},{4,0},{8,12},{12,8},{1,5},{5,1},{9,13},{13,9},{2,6},{6,2},{1... | collective-permute-start | bytes 1105928 | tf_op jit(solution)/shard_map/ppermute | solution.py:251
  68.9 0.7 copy-start.3
  78.7 0.8 copy-start.2
